TPU v7x, 256 devices: a whole 4x4x8 slice. The times are simulated.
256 devices in a mesh: feat: 64 (over z, y, core), layer: 4 (over x).
Axes of the slice: x: 4, y: 4, z: 8, core: 2. Of those that a mesh axis runs over, the one named last changes fastest.
Arguments:
- resid_in: bfloat16 [4, 512, 2304], P('layer', 'feat'), may hold values from -6 to 6
- enc_weight: bfloat16 [4, 2304, 32768], P('layer', None, 'feat'), may hold values from -0.125 to 0.125
- enc_bias: float32 [4, 32768], P('layer', 'feat'), may hold values from -3 to 3
- dec_weight: bfloat16 [4, 4, 32768, 2304], P('layer', None, 'feat'), may hold values from -0.03125 to 0.03125
- dec_bias: float32 [4, 2304], P('layer'), may hold values from -3 to 3
Outputs:
- recon: bfloat16 [4, 512, 2304], P('layer', 'feat')
All inputs are finite; a program needn't handle non-finite values.
Results may differ from a plain program's by a relative error of at most 0.0046.
Values may be sent and summed in bfloat16 or wider, within the bound.
A program may use at most 128 MiB of HBM per device.

v0:
```python
import jax
import jax.numpy as jnp
from jax import lax
from jax.sharding import Mesh
from jax.sharding import PartitionSpec as P

FEAT = ("feat_0", "feat_1", "feat_2")


def from_everyone(array, axis):
    copies = jnp.broadcast_to(array, (lax.axis_size(axis), *array.shape))
    return lax.all_to_all(copies, axis, split_axis=0, concat_axis=0, tiled=True)


def laid_out(blocks, dim):
    lengths = list(blocks.shape[1:])
    lengths[dim] *= blocks.shape[0]
    return jnp.moveaxis(blocks, 0, dim).reshape(lengths)


def gather_directly(array, axis, dim):
    blocks = from_everyone(array, axis)
    return laid_out(blocks, dim)


def sum_by_axis(array, axes, dim):
    for axis in axes:
        array = lax.psum_scatter(array, axis, scatter_dimension=dim, tiled=True)
    return array


def per_device(resid_in, enc_weight, enc_bias, dec_weight, dec_bias):
    preact = (
        jnp.dot(
            gather_directly(resid_in, FEAT, 1)[0], enc_weight[0], preferred_element_type=jnp.float32
        )
        + enc_bias[0][None, :]
    )
    actives = jnp.maximum(preact, 0.0).astype(jnp.bfloat16)[None]
    source = lax.axis_index("layer")
    total_rows = actives.shape[1]
    model_width = dec_weight.shape[3]
    incoming = lax.all_to_all(dec_weight, "layer", split_axis=1, concat_axis=0, tiled=True)
    every_actives = gather_directly(actives, "layer", 0)

    def accumulate(earlier, running):
        weight = lax.dynamic_index_in_dim(incoming, earlier, 0, keepdims=False)[0]
        rows = lax.dynamic_index_in_dim(every_actives, earlier, 0, keepdims=False)
        return running + jnp.dot(rows, weight, preferred_element_type=jnp.float32)

    start_sum = jnp.zeros((total_rows, model_width), jnp.float32)
    own_sum = lax.fori_loop(0, source + 1, accumulate, start_sum)
    summed = sum_by_axis(own_sum[None], FEAT, 1)
    return (summed + dec_bias[:, None, :]).astype(jnp.bfloat16)


def solution(mesh):
    finer = Mesh(
        mesh.devices.reshape(8, 4, 2, mesh.shape["layer"]), ("feat_0", "feat_1", "feat_2", "layer")
    )
    return jax.shard_map(
        per_device,
        mesh=finer,
        in_specs=(
            P("layer", FEAT, None),
            P("layer", None, FEAT),
            P("layer", FEAT),
            P("layer", None, FEAT, None),
            P("layer", None),
        ),
        out_specs=P("layer", FEAT, None),
        check_vma=False,
    )
```

profile of v0, /device:TPU:6, one launch (start us, length us, event | category | flops | bytes accessed | tf_op | source)
XLA Modules:
  0.0 352.7 jit_solution(7264707903136257638)
XLA Ops:
  6.5 1.1 broadcast_in_dim.15
  7.6 0.0 copy-start.2
  7.6 69.9 %all_to_all.22 = bf16[64,1,8,2304]{3,2,1,0:T(8,128)(2,1)S(1)} all-to-all(bf16[64,1,8,2304]{3,2,1,0:T(8,128)(2,1)S(1)} %broadcast_in_dim.15), channel_id=1, replica_groups=mesh['feat_0'=8,'feat_1'=4,'feat_2'=2,'layer'=4] {'feat_0','feat_1','fea..., dimensions={0} | all-to-all | bytes 4718592 | tf_op jit(solution)/shard_map/all_to_all | solution.py:12
  77.5 1.4 fusion.18
  78.9 0.2 broadcast_in_dim.16
  79.1 29.4 %all_to_all.23 = bf16[4,1,512,512]{3,2,1,0:T(8,128)(2,1)} all-to-all(bf16[4,1,512,512]{3,2,1,0:T(8,128)(2,1)S(1)} %broadcast_in_dim.16), channel_id=1, replica_groups=mesh['feat_0'=8,'feat_1'=4,'feat_2'=2,'layer'=4] {'layer'}, dimensions={0} | all-to-all | bytes 4194304 | tf_op jit(solution)/shard_map/all_to_all | solution.py:12
  108.5 7.8 %all-to-all-start.2 = ((bf16[1,4,512,2304]{3,2,0,1:T(8,128)(2,1)}), bf16[1,4,512,2304]{3,2,0,1:T(8,128)(2,1)}, u32[]{:S(2)}, u32[]{:S(2)}) async-start(bf16[1,4,512,2304]{3,2,0,1:T(8,128)(2,1)} %bitcast.38), calls=%async_computation.2 | async-start | bytes 18874368 | tf_op jit(solution)/shard_map/all_to_all | solution.py:43
  116.3 0.0 reduce-scatter.4.cloned.1.call-start
  116.3 102.6 %all-to-all-done.2 = bf16[1,4,512,2304]{3,2,0,1:T(8,128)(2,1)} async-done(((bf16[1,4,512,2304]{3,2,0,1:T(8,128)(2,1)}), bf16[1,4,512,2304]{3,2,0,1:T(8,128)(2,1)}, u32[]{:S(2)}, u32[]{:S(2)}) %all-to-all-start.2) | async-done | bytes 9437216 | tf_op jit(solution)/shard_map/all_to_all | solution.py:43
  219.0 2.6 broadcast_in_dim.14
  221.5 27.4 %while.10 = (s32[]{:T(128)}, f32[512,2304]{1,0:T(8,128)}, s32[]{:T(128)}, bf16[4,512,512]{2,1,0:T(8,128)(2,1)}, bf16[4,1,512,2304]{3,2,1,0:T(8,128)(2,1)}, /*index=5*/s32[]{:T(128)}, s32[]{:T(128)}, s32[]{:T(128)}) while((s32[]{:T(128)}, f32[512,2304]{1,0:T(8,128)}, s32[]{:T(128)}, bf16[4,512,512]{2,1,0:T(8,128)(2,1)}, ...), condition=%wide.region_1.2_spmd, body=%wide.region_0.1_spmd.sunk | while | flops 1209139200 | bytes 12321911 | solution.py:52
  221.5 6.9 %convolution_add_fusion.2 = f32[512,2304]{1,0:T(8,128)} fusion(f32[512,2304]{1,0:T(8,128)} %get-tuple-element.90, bf16[4,1,512,2304]{3,2,1,0:T(8,128)(2,1)} %get-tuple-element.101, s32[]{:T(128)S(6)} %select_n.7, bf16[4,512,512]{2,1,0:T(8,128)(2,1)} %get-tuple-element.100), kind=kOutput, calls=%fused_computation.clone.1 | convolution fusion | flops 1209139200 | bytes 12321792 | tf_op jit(solution)/shard_map/while/body/dot_general | solution.py:49
  228.4 6.9 %convolution_add_fusion.2 = f32[512,2304]{1,0:T(8,128)} fusion(f32[512,2304]{1,0:T(8,128)} %get-tuple-element.90, bf16[4,1,512,2304]{3,2,1,0:T(8,128)(2,1)} %get-tuple-element.101, s32[]{:T(128)S(6)} %select_n.7, bf16[4,512,512]{2,1,0:T(8,128)(2,1)} %get-tuple-element.100), kind=kOutput, calls=%fused_computation.clone.1 | convolution fusion | flops 1209139200 | bytes 12321792 | tf_op jit(solution)/shard_map/while/body/dot_general | solution.py:49
  235.2 6.9 %convolution_add_fusion.2 = f32[512,2304]{1,0:T(8,128)} fusion(f32[512,2304]{1,0:T(8,128)} %get-tuple-element.90, bf16[4,1,512,2304]{3,2,1,0:T(8,128)(2,1)} %get-tuple-element.101, s32[]{:T(128)S(6)} %select_n.7, bf16[4,512,512]{2,1,0:T(8,128)(2,1)} %get-tuple-element.100), kind=kOutput, calls=%fused_computation.clone.1 | convolution fusion | flops 1209139200 | bytes 12321792 | tf_op jit(solution)/shard_map/while/body/dot_general | solution.py:49
  242.1 6.9 %convolution_add_fusion.2 = f32[512,2304]{1,0:T(8,128)} fusion(f32[512,2304]{1,0:T(8,128)} %get-tuple-element.90, bf16[4,1,512,2304]{3,2,1,0:T(8,128)(2,1)} %get-tuple-element.101, s32[]{:T(128)S(6)} %select_n.7, bf16[4,512,512]{2,1,0:T(8,128)(2,1)} %get-tuple-element.100), kind=kOutput, calls=%fused_computation.clone.1 | convolution fusion | flops 1209139200 | bytes 12321792 | tf_op jit(solution)/shard_map/while/body/dot_general | solution.py:49
  249.0 0.0 reduce-scatter.4.cloned.1.call-update
  249.0 0.0 reduce-scatter.6.cloned.1.call-start
  249.0 54.9 %reduce-scatter.4.cloned.1.call-done = f32[1,64,2304]{2,1,0:T(8,128)} async-done(((f32[1,512,2304]{2,1,0:T(8,128)}), f32[1,64,2304]{2,1,0:T(8,128)}) %reduce-scatter.4.cloned.1.call-update) | async-done | bytes 589840 | tf_op jit(solution)/shard_map/reduce_scatter | solution.py:28
  303.9 0.0 reduce-scatter.6.cloned.1.call-update
  303.9 0.0 reduce-scatter.8.cloned.1.call-start
  304.0 25.5 %reduce-scatter.6.cloned.1.call-done = f32[1,16,2304]{2,1,0:T(8,128)} async-done(((f32[1,64,2304]{2,1,0:T(8,128)}), f32[1,16,2304]{2,1,0:T(8,128)}) %reduce-scatter.6.cloned.1.call-update) | async-done | bytes 147472 | tf_op jit(solution)/shard_map/reduce_scatter | solution.py:28
  329.5 0.0 reduce-scatter.8.cloned.1.call-update
  329.6 15.1 %reduce-scatter.8.cloned.1.call-done = f32[1,8,2304]{2,1,0:T(8,128)} async-done(((f32[1,16,2304]{2,1,0:T(8,128)}), f32[1,8,2304]{2,1,0:T(8,128)}) %reduce-scatter.8.cloned.1.call-update) | async-done | bytes 73744 | tf_op jit(solution)/shard_map/reduce_scatter | solution.py:28
  344.6 1.5 add_convert_fusion
  (6 shorter events, 0.0 us)
Async XLA Ops:
  6.5 71.0 %copy-start = (bf16[1,2304,512]{2,1,0:T(8,128)(2,1)S(1)}, bf16[1,2304,512]{2,1,0:T(8,128)(2,1)}, u32[]{:S(2)}) copy-start(bf16[1,2304,512]{2,1,0:T(8,128)(2,1)} %param.8) | copy-start | bytes 7077892
  7.6 69.9 %copy-start.2 = (f32[1,512]{1,0:T(1,128)S(1)}, f32[1,512]{1,0:T(1,128)}, u32[]{:S(2)}) copy-start(f32[1,512]{1,0:T(1,128)} %param.9) | copy-start | bytes 6148
  108.5 110.5 %all-to-all-start.2 = ((bf16[1,4,512,2304]{3,2,0,1:T(8,128)(2,1)}), bf16[1,4,512,2304]{3,2,0,1:T(8,128)(2,1)}, u32[]{:S(2)}, u32[]{:S(2)}) async-start(bf16[1,4,512,2304]{3,2,0,1:T(8,128)(2,1)} %bitcast.38), calls=%async_computation.2 | async-start | bytes 18874368 | tf_op jit(solution)/shard_map/all_to_all | solution.py:43
  116.3 187.6 %reduce-scatter.4.cloned.1.call-start = ((), (), s32[]{:S(2)}) async-start(), calls=%async_computation.6 | async-start | bytes 5308416 | tf_op jit(solution)/shard_map/reduce_scatter | solution.py:28
  249.0 80.6 %copy-start.1 = (f32[1,2304]{1,0:T(1,128)S(1)}, f32[1,2304]{1,0:T(1,128)}, u32[]{:S(2)}) copy-start(f32[1,2304]{1,0:T(1,128)} %param.11) | copy-start | bytes 27652
  249.0 80.5 %reduce-scatter.6.cloned.1.call-start = ((), (), s32[]{:S(2)}) async-start(), calls=%async_computation.7 | async-start | bytes 737280 | tf_op jit(solution)/shard_map/reduce_scatter | solution.py:28
  303.9 40.7 %reduce-scatter.8.cloned.1.call-start = ((), (), s32[]{:S(2)}) async-start(), calls=%async_computation.8 | async-start | bytes 221184 | tf_op jit(solution)/shard_map/reduce_scatter | solution.py:28
Sparse Core Ops, SparseCore 0:
  249.1 54.7 reduce-scatter.3
  306.4 23.0 reduce-scatter.5
  332.0 12.6 reduce-scatter.7
where the time goes:
time: 355 us; the launch traced here: 353 us
  waiting for transfers between devices  198 us (56%)
  blocking collectives  99.3 us (28%)
  matrix products  28.8 us (8%)
  between operations  13.1 us (4%)
  starting transfers between devices  7.93 us (2%)
  local copies, waits for them, and re-layouts  3.8 us (1%)
    all_to_all x1, waiting for transfers between devices, per_device(): lax.all_to_all(dec_weight, 'layer', split_axis=1, concat_axis=0, tiled=True)  103 us
    all_to_all x2, blocking collectives, from_everyone(): return lax.all_to_all(copies, axis, split_axis=0, concat_axis=0, tiled=True)  99.3 us
    reduce_scatter x3, waiting for transfers between devices, sum_by_axis(): array = lax.psum_scatter(array, axis, scatter_dimension=dim, tiled=True)  95.5 us
    dot_general x4, matrix products, accumulate(): return running + jnp.dot(rows, weight, preferred_element_type=jnp.float32)  27.4 us
    all_to_all x1, starting transfers between devices, per_device(): lax.all_to_all(dec_weight, 'layer', split_axis=1, concat_axis=0, tiled=True)  7.85 us
  transfers between devices with their start and end apart: 4, of which 4 were waited for; matrix products, arithmetic and copies ran while one was open for 0% of the time, Pallas kernels for 0%

commit v1 on v0

v1 whole, which is shorter than its diff:
```python
import jax
import jax.numpy as jnp
from jax import lax
from jax.experimental import pallas as pl
from jax.experimental.pallas import tpu as pltpu
from jax.sharding import Mesh
from jax.sharding import PartitionSpec as P

FEAT = ("z", "y", "c")
MESH = pl.DeviceIdType.MESH
Z, Y, C, X = 8, 4, 2, 4
SIZE = {"z": Z, "y": Y, "c": C, "x": X}
ROWS = 8
D = 2304
FEATS = 512
TILE = 256
GATHER_SPLIT = 1152
B_COLS = 1280
A_COLS = D - B_COLS


class Group:
    def __init__(self, first, start, width, ks):
        self.first, self.second = first, "y" if first == "z" else "z"
        self.start, self.width, self.ks = start, width, ks
        self.n1, self.n2 = SIZE[self.first], SIZE[self.second]

    def scratch(self):
        k, n1, n2, w = self.ks, self.n1, self.n2, self.width
        return [
            pltpu.VMEM((k, n1 - 1, n2, ROWS, w), jnp.bfloat16),
            pltpu.VMEM((k, n1 - 1, n2, ROWS, w), jnp.bfloat16),
            pltpu.VMEM((k, n2, ROWS, w), jnp.float32),
            pltpu.VMEM((k, n2 - 1, ROWS, w), jnp.bfloat16),
            pltpu.VMEM((k, n2 - 1, ROWS, w), jnp.bfloat16),
            pltpu.SemaphoreType.DMA((k, n1 - 1)),
            pltpu.SemaphoreType.DMA((k, n1 - 1)),
            pltpu.SemaphoreType.DMA((k, n2 - 1)),
            pltpu.SemaphoreType.DMA((k, n2 - 1)),
        ]

    def bind(self, refs):
        (self.s1, self.r1, self.t, self.s2, self.r2, self.ss1, self.rs1, self.ss2, self.rs2) = refs


def groups():
    return [
        Group("y", 0, 768, 4),
        Group("z", 768, 512, 4),
        Group("y", B_COLS, 512, 2),
        Group("z", B_COLS + 512, 512, 2),
    ]


def shifted(axis, step):
    return lax.rem(lax.axis_index(axis) + step + 2 * SIZE[axis], SIZE[axis])


def remote(src, dst, send, recv, axis, step):
    return pltpu.make_async_remote_copy(
        src_ref=src, dst_ref=dst, send_sem=send, recv_sem=recv,
        device_id={axis: shifted(axis, step)}, device_id_type=MESH,
    )


def kernel(x_ref, enc_ref, eb_ref, dec_ref, db_ref, o_ref, wenc, wdec, ebv, xg, act, part, mvs, mvr, fin, fsend, frecv,
           local_sem, w_ss, w_rs, ay_ss, ay_rs, az_ss, az_rs, bz_ss, bz_rs, by_ss, by_rs, mv_ss, mv_rs, f_ss, f_rs, *rest):
    gs = groups()
    for i, g in enumerate(gs):
        g.bind(rest[9 * i : 9 * i + 9])
    z, y, c, l = (lax.axis_index(a) for a in ("z", "y", "c", "x"))
    n_b = X - l
    n_a = jnp.where(l < 2, 2, 1)

    locals_ = [
        pltpu.make_async_copy(enc_ref.at[0], wenc.at[c], local_sem.at[0]),
        pltpu.make_async_copy(eb_ref, ebv.at[c], local_sem.at[1]),
        pltpu.make_async_copy(x_ref.at[0], xg.at[y, z], local_sem.at[2]),
    ]
    for cp in locals_:
        cp.start()

    def dec_local(k):
        return pltpu.make_async_copy(dec_ref.at[0, l + k], wdec.at[k, c], local_sem.at[3 + k])

    def dec_push(k):
        return remote(dec_ref.at[0, l + k], wdec.at[k, c], w_ss.at[2 + k], w_rs.at[2 + k], "c", 1)

    def each_k(fn, order=(1, 3, 0, 2)):
        for k in order:
            if k == 0:
                fn(0)
            else:
                pl.when(l + k < X)(lambda k=k: fn(k))

    each_k(lambda k: dec_local(k).start())

    bar = pltpu.get_barrier_semaphore()
    peers = [("c", 1)] + [("y", i) for i in (1, 2, 3)] + [("z", i) for i in range(1, 8)] + [("x", i) for i in (1, 2, 3)]
    for a, i in peers:
        pl.semaphore_signal(bar, inc=1, device_id={a: shifted(a, i)}, device_id_type=MESH)
    pl.semaphore_wait(bar, len(peers))

    lo, hi = pl.ds(0, GATHER_SPLIT), pl.ds(GATHER_SPLIT, D - GATHER_SPLIT)

    def gy(i):
        return remote(x_ref.at[0, :, lo], xg.at[y, z, :, lo], ay_ss.at[i - 1], ay_rs.at[i - 1], "y", i)

    def gz(i):
        return remote(x_ref.at[0, :, hi], xg.at[y, z, :, hi], bz_ss.at[i - 1], bz_rs.at[i - 1], "z", i)

    def chain(s, j, long):
        step = (1 if long else -1) * (1 if j % 2 == 0 else -1)
        zb = shifted("z", -step * s)
        yb = shifted("y", -j)
        slot = (s if long else 4 + s) * 4 + j
        src = x_ref.at[0, :, lo] if s == 0 and j == 0 else xg.at[yb, zb, :, lo]
        return remote(src, xg.at[yb, zb, :, lo], az_ss.at[slot], az_rs.at[slot], "z", step)

    def hop(s, j):
        for long, hops in ((True, 4), (False, 3)):
            if s > 0 and s <= hops:
                chain(s - 1, j, long).wait_recv()
            if s < hops:
                chain(s, j, long).start()

    def across(j, i):
        zb = shifted("z", -j)
        src = x_ref.at[0, :, hi] if j == 0 else xg.at[y, zb, :, hi]
        return remote(src, xg.at[y, zb, :, hi], by_ss.at[j * 3 + i - 1], by_rs.at[j * 3 + i - 1], "y", i)

    def spread(j):
        for i in (1, 3, 2):
            across(j, i).start()

    for i in (1, 3, 2):
        gy(i).start()
    for i in (4, 3, 5, 2, 6, 1, 7):
        gz(i).start()
    hop(0, 0)
    spread(0)

    enc_push = remote(enc_ref.at[0], wenc.at[c], w_ss.at[0], w_rs.at[0], "c", 1)
    eb_push = remote(eb_ref, ebv.at[c], w_ss.at[1], w_rs.at[1], "c", 1)
    enc_push.start()
    eb_push.start()
    each_k(lambda k: dec_push(k).start())

    def take_y(i):
        gy(i).wait_recv()
        hop(0, i)

    def take_z(j):
        gz(j).wait_recv()
        spread(j)

    take_y(1), take_y(3), take_z(1), take_z(7), hop(1, 0), take_y(2), take_z(2), take_z(6), hop(1, 1), hop(1, 3)
    take_z(3), take_z(5), hop(1, 2), take_z(4)
    for s in (2, 3, 4):
        for j in (0, 1, 3, 2):
            hop(s, j)
    for j in (0, 1, 7, 2, 6, 3, 5, 4):
        for i in (1, 3, 2):
            across(j, i).wait_recv()
    for cp in locals_:
        cp.wait()
    enc_push.wait_recv()
    eb_push.wait_recv()

    rows = xg[...].astype(jnp.float32).reshape(Z * Y * ROWS, D).astype(jnp.bfloat16)
    for side in range(C):
        for n in range(FEATS // TILE):
            at = pl.ds(n * TILE, TILE)
            pre = jnp.dot(rows, wenc[side, :, at], preferred_element_type=jnp.float32) + ebv[side, :, at]
            act[:, pl.ds(side * FEATS + n * TILE, TILE)] = jnp.maximum(pre, 0.0).astype(jnp.bfloat16)

    def product(k, col):
        at = pl.ds(col, TILE)
        weight = wdec[k, :, :, at].reshape(C * FEATS, TILE)
        out = jnp.dot(act[...], weight, preferred_element_type=jnp.float32)
        return out.reshape(Y, Z, ROWS, TILE)

    def dec_ready(k):
        dec_local(k).wait()
        dec_push(k).wait_recv()

    def move(i, n):
        at = pl.ds(n * TILE, TILE)
        return remote(mvs.at[i, :, :, :, at], mvr.at[i, :, :, :, at], mv_ss.at[i, n], mv_rs.at[i, n], "x", 1 - 2 * i)

    def moved(k):
        dec_ready(k)
        i = k // 2
        for n in range(A_COLS // TILE):
            mvs[i, :, :, :, pl.ds(n * TILE, TILE)] = product(k, B_COLS + n * TILE).astype(jnp.bfloat16)
            move(i, n).start()

    each_k(moved, (1, 3))

    def own1(g, k, d):
        cols = pl.ds(g.start, g.width)
        return part[k, d, :, :, cols] if g.first == "y" else part[k, :, d, :, cols]

    def own2(g, j, d):
        return g.t[j, d]

    def send_copy(g, stage, j, slot, step):
        s, r, ss, rs = (g.s1, g.r1, g.ss1, g.rs1) if stage == 1 else (g.s2, g.r2, g.ss2, g.rs2)
        return remote(s.at[j, slot], r.at[j, slot], ss.at[j, slot], rs.at[j, slot], g.first if stage == 1 else g.second, step)

    def ring(g, stage, j, k, s):
        axis, size = (g.first, g.n1) if stage == 1 else (g.second, g.n2)
        own = (lambda d: own1(g, k, d)) if stage == 1 else (lambda d: own2(g, j, d))
        sref, rref = (g.s1, g.r1) if stage == 1 else (g.s2, g.r2)
        sign = 1 - 2 * lax.rem(j, 2)
        half = size // 2
        for hops, step, base in ((half, sign, 0), (half - 1, -sign, half)):
            if s > 0 and s <= hops:
                send_copy(g, stage, j, base + s - 1, step).wait_recv()
            if s < hops:
                msg = own(shifted(axis, step * (hops - s)))
                if s > 0:
                    msg = msg + rref[j, base + s - 1].astype(jnp.float32)
                sref[j, base + s] = msg.astype(jnp.bfloat16)
                send_copy(g, stage, j, base + s, step).start()
        if s == half:
            me = lax.axis_index(axis)
            total = own(me) + rref[j, half - 1].astype(jnp.float32) + rref[j, size - 2].astype(jnp.float32)
            if stage == 1:
                g.t[j] = total
            else:
                fin[k, :, pl.ds(g.start, g.width)] = total

    def direct_send(g, j):
        for o in range(1, g.n2):
            g.s2[j, o - 1] = own2(g, j, shifted(g.second, o)).astype(jnp.bfloat16)
            send_copy(g, 2, j, o - 1, o).start()

    def direct_sum(g, j, k):
        total = own2(g, j, lax.axis_index(g.second))
        for o in range(1, g.n2):
            send_copy(g, 2, j, o - 1, o).wait_recv()
            total = total + g.r2[j, o - 1].astype(jnp.float32)
        fin[k, :, pl.ds(g.start, g.width)] = total

    by, bz, ay, az = gs

    def loop_b(fn):
        def body(k, carry):
            fn(k)
            return carry

        lax.fori_loop(0, n_b, body, 0)

    def loop_a(fn):
        def body(j, carry):
            fn(j, 2 * j)
            return carry

        lax.fori_loop(0, n_a, body, 0)

    def compute_b(k):
        for n in range(B_COLS // TILE):
            part[k, :, :, :, pl.ds(n * TILE, TILE)] = product(k, n * TILE)
        ring(by, 1, k, k, 0)
        ring(bz, 1, k, k, 0)

    def first_b(k):
        @pl.when(lax.rem(k, 2) == 0)
        def _():
            dec_ready(k)

        compute_b(k)

    loop_b(first_b)

    def compute_a(j, k):
        for n in range(A_COLS // TILE):
            at = B_COLS + n * TILE
            part[k, :, :, :, pl.ds(at, TILE)] = product(k, at)

    loop_a(compute_a)

    @pl.when(l < 2)
    def _():
        ring(ay, 1, 1, 2, 0)
        ring(az, 1, 1, 2, 0)

    def step_b(s):
        def fn(k):
            if s <= 2:
                ring(by, 1, k, k, s)
            ring(bz, 1, k, k, s)
            if s == 2:
                ring(by, 2, k, k, 0)
            if s == 4:
                ring(bz, 2, k, k, 0)

        loop_b(fn)

    step_b(1)
    step_b(2)

    def join(i):
        for n in range(A_COLS // TILE):
            move(i, n).wait_recv()
            at = pl.ds(B_COLS + n * TILE, TILE)
            part[0, :, :, :, at] = part[0, :, :, :, at] + mvr[i, :, :, :, pl.ds(n * TILE, TILE)].astype(jnp.float32)

    pl.when(l > 0)(lambda: join(0))
    pl.when(l == X - 1)(lambda: join(1))
    ring(ay, 1, 0, 0, 0)
    ring(az, 1, 0, 0, 0)

    step_b(3)
    step_b(4)

    def step_a(s):
        def fn(j, k):
            if s <= 2:
                ring(ay, 1, j, k, s)
            ring(az, 1, j, k, s)
            if s == 2:
                direct_send(ay, j)
            if s == 4:
                direct_send(az, j)

        loop_a(fn)

    def tail_b(s):
        def fn(k):
            ring(by, 2, k, k, s)
            if s <= 2:
                ring(bz, 2, k, k, s)

        loop_b(fn)

    for s in (1, 2, 3, 4):
        step_a(s)
        tail_b(s)

    def late(k, is_a):
        at = pl.ds(B_COLS, A_COLS) if is_a else pl.ds(0, B_COLS)
        slot = 3 if is_a else k - 1
        return remote(fsend.at[k - 1, :, at], frecv.at[k - 1, :, at], f_ss.at[slot], f_rs.at[slot], "x", k)

    def send_late(k, is_a):
        at = pl.ds(B_COLS, A_COLS) if is_a else pl.ds(0, B_COLS)
        fsend[k - 1, :, at] = fin[k, :, at].astype(jnp.bfloat16)
        late(k, is_a).start()

    each_k(lambda k: send_late(k, False), (1, 2, 3))

    def end_a(j, k):
        direct_sum(ay, j, k)
        direct_sum(az, j, k)

    loop_a(end_a)
    pl.when(l < 2)(lambda: send_late(2, True))

    def take_late(k, is_a):
        late(k, is_a).wait_recv()
        at = pl.ds(B_COLS, A_COLS) if is_a else pl.ds(0, B_COLS)
        fin[0, :, at] = fin[0, :, at] + frecv[k - 1, :, at].astype(jnp.float32)

    for k in (1, 2, 3):
        pl.when(l >= k)(lambda k=k: take_late(k, False))
    pl.when(l >= 2)(lambda: take_late(2, True))
    o_ref[0] = (fin[0] + db_ref[...]).astype(jnp.bfloat16)

    for i in (1, 2, 3):
        gy(i).wait_send()
        for j in range(Z):
            across(j, i).wait_send()
    for i in range(1, Z):
        gz(i).wait_send()
    for j in range(Y):
        for s in range(4):
            chain(s, j, True).wait_send()
            if s < 3:
                chain(s, j, False).wait_send()
    enc_push.wait_send()
    eb_push.wait_send()
    each_k(lambda k: dec_push(k).wait_send())

    def moves_left(k):
        for n in range(A_COLS // TILE):
            move(k // 2, n).wait_send()

    each_k(moves_left, (1, 3))
    each_k(lambda k: late(k, False).wait_send(), (1, 2, 3))
    pl.when(l < 2)(lambda: late(2, True).wait_send())

    def drain(g, j):
        for slot in range(g.n1 - 1):
            send_copy(g, 1, j, slot, 1).wait_send()
        for slot in range(g.n2 - 1):
            send_copy(g, 2, j, slot, 1).wait_send()

    loop_b(lambda k: (drain(by, k), drain(bz, k)))
    loop_a(lambda j, k: (drain(ay, j), drain(az, j)))


def per_device(resid_in, enc_weight, enc_bias, dec_weight, dec_bias):
    dma = pltpu.SemaphoreType.DMA
    scratch = [
        pltpu.VMEM((C, D, FEATS), jnp.bfloat16),
        pltpu.VMEM((X, C, FEATS, D), jnp.bfloat16),
        pltpu.VMEM((C, 1, FEATS), jnp.float32),
        pltpu.VMEM((Y, Z, ROWS, D), jnp.bfloat16),
        pltpu.VMEM((Z * Y * ROWS, C * FEATS), jnp.bfloat16),
        pltpu.VMEM((X, Y, Z, ROWS, D), jnp.float32),
        pltpu.VMEM((2, Y, Z, ROWS, A_COLS), jnp.bfloat16),
        pltpu.VMEM((2, Y, Z, ROWS, A_COLS), jnp.bfloat16),
        pltpu.VMEM((X, ROWS, D), jnp.float32),
        pltpu.VMEM((X - 1, ROWS, D), jnp.bfloat16),
        pltpu.VMEM((X - 1, ROWS, D), jnp.bfloat16),
        dma((7,)),
        dma((6,)), dma((6,)),
        dma((3,)), dma((3,)),
        dma((28,)), dma((28,)),
        dma((7,)), dma((7,)),
        dma((24,)), dma((24,)),
        dma((2, A_COLS // TILE)), dma((2, A_COLS // TILE)),
        dma((4,)), dma((4,)),
    ]
    for g in groups():
        scratch += g.scratch()
    anywhere = pl.BlockSpec(memory_space=pl.ANY)
    return pl.pallas_call(
        kernel,
        out_shape=jax.ShapeDtypeStruct((1, ROWS, D), jnp.bfloat16),
        in_specs=[anywhere, anywhere, anywhere, anywhere, pl.BlockSpec(memory_space=pltpu.VMEM)],
        out_specs=pl.BlockSpec(memory_space=pltpu.VMEM),
        scratch_shapes=scratch,
        compiler_params=pltpu.CompilerParams(collective_id=0, has_side_effects=True, vmem_limit_bytes=67043328),
        name="transcoder",
    )(resid_in, enc_weight, enc_bias, dec_weight, dec_bias)


def solution(mesh):
    finer = Mesh(mesh.devices.reshape(Z, Y, C, X), ("z", "y", "c", "x"))
    return jax.shard_map(
        per_device,
        mesh=finer,
        in_specs=(
            P("x", FEAT, None),
            P("x", None, FEAT),
            P("x", FEAT),
            P("x", None, FEAT, None),
            P("x", None),
        ),
        out_specs=P("x", FEAT, None),
        check_vma=False,
    )
```

time: 355 us -> 76.9 us (0.22)
  the two profiles are of different devices: /device:TPU:6 before, /device:TPU:4 now
where the time goes in v1:
time: 76.9 us; the launch traced here: 76.7 us
  Pallas kernels  75.3 us (98%)
  local copies, waits for them, and re-layouts  1.39 us (2%)
    pallas_call x1, Pallas kernels, per_device(): pl.pallas_call(kernel, out_shape=jax.ShapeDtypeStruct((1, ROWS, D), jnp.b...  75.3 us

profile of v1, /device:TPU:4, one launch (start us, length us, event | category | flops | bytes accessed | tf_op | source)
XLA Modules:
  0.0 76.7 jit_solution(17329749436939408574)
XLA Ops:
  0.0 75.3 %transcoder.1 = bf16[1,8,2304]{2,1,0:T(8,128)(2,1)} custom-call(bf16[1,8,2304]{2,1,0:T(8,128)(2,1)} %x_ref.1, bf16[1,2304,512]{2,1,0:T(8,128)(2,1)} %enc_ref.1, f32[1,512]{1,0:T(1,128)} %eb_ref.1, bf16[1,4,512,2304]{3,2,1,0:T(8,128)(2,1)} %dec_ref.1, f32[1,2304]{1,0:T(1,128)} %db_ref.1), custom_call_target="tpu_custom_call" | custom-call | tf_op jit(solution)/shard_map/transcoder/pallas_call | solution.py:430
  75.3 1.4 %copy.7 = bf16[1,8,2304]{2,1,0:T(8,128)(2,1)} copy(bf16[1,8,2304]{2,1,0:T(8,128)(2,1)} %transcoder.1) | data formatting | bytes 73728

commit v2 on v1

v2 whole, which is shorter than its diff:
```python
import jax
import jax.numpy as jnp
from jax import lax
from jax.experimental import pallas as pl
from jax.experimental.pallas import tpu as pltpu
from jax.sharding import Mesh
from jax.sharding import PartitionSpec as P

FEAT = ("z", "y", "c")
MESH = pl.DeviceIdType.MESH
Z, Y, C, X = 8, 4, 2, 4
SIZE = {"z": Z, "y": Y, "c": C, "x": X}
ROWS = 8
D = 2304
FEATS = 512
TILE = 256
GATHER_SPLIT = 896
B_COLS = 1280
A_COLS = D - B_COLS

ORDER = (
    (1,1), (1,3), (0,1), (0,2), (2,2), (0,3), (0,0), (4,1,1,1,1,1), (4,1,1,1,0,1), (4,0,1,1,1,1), (4,0,1,1,0,1), (2,0), (4,1,1,2,1,1),
    (4,1,1,2,0,1), (4,0,1,2,1,1), (4,0,1,2,0,1), (4,1,1,3,1,1), (4,1,1,3,0,1), (4,1,1,0,1,1), (4,1,1,0,0,1), (4,2,1,2,1,1),
    (4,2,1,2,0,1), (4,1,1,1,1,2), (4,1,1,1,0,2), (4,1,1,2,1,2), (4,1,1,2,0,2), (4,0,1,3,1,1), (4,0,1,3,0,1), (4,1,1,3,1,2),
    (4,1,1,3,0,2), (3,2), (4,0,1,0,1,1), (4,0,1,0,0,1), (4,1,1,0,1,2), (4,1,1,0,0,2), (4,0,1,1,1,2), (4,0,1,2,1,2), (4,1,1,1,1,3),
    (4,1,1,1,0,3), (4,1,1,2,1,3), (4,1,1,2,0,3), (4,1,1,3,1,3), (4,1,1,3,0,3), (4,2,1,2,1,2), (4,1,1,0,1,3), (4,1,1,0,0,3),
    (4,2,1,0,1,1), (4,0,1,3,1,2), (4,0,1,0,1,2), (5,0,1), (4,2,1,0,0,1), (4,1,1,1,1,4), (4,1,1,2,1,4), (5,0,2), (4,1,1,3,1,4),
    (4,2,1,0,1,2), (4,1,1,0,1,4), (5,1,1), (5,1,2), (5,1,3), (5,2,2), (5,1,0), (5,0,3), (5,0,0), (5,2,0),
)

class Group:
    def __init__(self, first, start, width, ks, direct):
        self.first, self.second = first, "y" if first == "z" else "z"
        self.start, self.width, self.ks = start, width, ks
        self.n1, self.n2 = SIZE[self.first], SIZE[self.second]
        self.direct = direct

    def scratch(self):
        k, n1, n2, w = self.ks, self.n1, self.n2, self.width
        return [
            pltpu.VMEM((k, n1 - 1, n2, ROWS, w), jnp.bfloat16),
            pltpu.VMEM((k, n1 - 1, n2, ROWS, w), jnp.bfloat16),
            pltpu.VMEM((k, n2, ROWS, w), jnp.float32),
            pltpu.VMEM((k, n2 - 1, ROWS, w), jnp.bfloat16),
            pltpu.VMEM((k, n2 - 1, ROWS, w), jnp.bfloat16),
            pltpu.SemaphoreType.DMA((k,)),
            pltpu.SemaphoreType.DMA((k, n1 - 1)),
            pltpu.SemaphoreType.DMA((k,)),
            pltpu.SemaphoreType.DMA((k, 1 if self.direct else n2 - 1)),
        ]

    def bind(self, refs):
        (self.s1, self.r1, self.t, self.s2, self.r2, self.ss1, self.rs1, self.ss2, self.rs2) = refs


def groups():
    return [
        Group("y", 0, 512, 4, True),
        Group("z", 512, 768, 4, True),
        Group("y", 1280, 1024, 2, True),
    ]


def shifted(axis, step):
    return lax.rem(lax.axis_index(axis) + step + 2 * SIZE[axis], SIZE[axis])


def remote(src, dst, send, recv, axis, step):
    return pltpu.make_async_remote_copy(
        src_ref=src, dst_ref=dst, send_sem=send, recv_sem=recv,
        device_id={axis: shifted(axis, step)}, device_id_type=MESH,
    )


def kernel(x_ref, enc_ref, eb_ref, dec_ref, db_ref, o_ref, wenc, wdec, ebv, xg, act, part, mvs, mvr, fin, fsend, frecv,
           local_sem, w_ss, w_rs, ay_ss, ay_rs, az_ss, az_rs, bz_ss, bz_rs, by_ss, by_rs, mv_ss, mv_rs, f_ss, f_rs, partner_sem, *rest):
    gs = groups()
    for i, g in enumerate(gs):
        g.bind(rest[9 * i : 9 * i + 9])
    z, y, c, l = (lax.axis_index(a) for a in ("z", "y", "c", "x"))

    locals_ = [
        pltpu.make_async_copy(enc_ref.at[0], wenc.at[c], local_sem.at[0]),
        pltpu.make_async_copy(eb_ref, ebv.at[c], local_sem.at[1]),
        pltpu.make_async_copy(x_ref.at[0], xg.at[y, z], local_sem.at[2]),
    ]
    for cp in locals_:
        cp.start()

    def dec_local(k):
        return pltpu.make_async_copy(dec_ref.at[0, l + k], wdec.at[k, c], local_sem.at[3 + k])

    def dec_push(k):
        return remote(dec_ref.at[0, l + k], wdec.at[k, c], w_ss.at[2 + k], w_rs.at[2 + k], "c", 1)

    def each_k(fn, order=(1, 3, 2, 0)):
        for k in order:
            if k == 0:
                fn(0)
            else:
                pl.when(l + k < X)(lambda k=k: fn(k))

    each_k(lambda k: dec_local(k).start())

    bar = pltpu.get_barrier_semaphore()
    peers = [("y", i) for i in (1, 2, 3)] + [("z", i) for i in range(1, 8)] + [("x", i) for i in (1, 2, 3)]

    @pl.when(c == 0)
    def _():
        pl.semaphore_signal(bar, inc=1, device_id={"c": 1}, device_id_type=MESH)

    for a, i in peers:
        pl.semaphore_signal(bar, inc=1, device_id={a: shifted(a, i)}, device_id_type=MESH)
    pl.semaphore_wait(bar, len(peers) + c)

    @pl.when(c == 1)
    def _():
        pl.semaphore_signal(partner_sem, inc=1, device_id={"c": 0}, device_id_type=MESH)

    lo, hi = pl.ds(0, GATHER_SPLIT), pl.ds(GATHER_SPLIT, D - GATHER_SPLIT)

    def gy(i):
        return remote(x_ref.at[0, :, lo], xg.at[y, z, :, lo], ay_ss.at[0], ay_rs.at[i - 1], "y", i)

    def gz(i):
        return remote(x_ref.at[0, :, hi], xg.at[y, z, :, hi], bz_ss.at[0], bz_rs.at[i - 1], "z", i)

    def along(j, i):
        yb = shifted("y", -j)
        src = x_ref.at[0, :, lo] if j == 0 else xg.at[yb, z, :, lo]
        return remote(src, xg.at[yb, z, :, lo], az_ss.at[0], az_rs.at[i - 1], "z", i)

    far_first = (4, 3, 5, 2, 6, 1, 7)

    def spread_z(j):
        for i in far_first:
            along(j, i).start()

    def across(j, i):
        zb = shifted("z", -j)
        src = x_ref.at[0, :, hi] if j == 0 else xg.at[y, zb, :, hi]
        return remote(src, xg.at[y, zb, :, hi], by_ss.at[0], by_rs.at[i - 1], "y", i)

    def spread(j):
        for i in (1, 3, 2):
            across(j, i).start()

    for i in (1, 3, 2):
        gy(i).start()
    for i in far_first:
        gz(i).start()
    spread(0)
    spread_z(0)

    enc_push = remote(enc_ref.at[0], wenc.at[c], w_ss.at[0], w_rs.at[0], "c", 1)
    eb_push = remote(eb_ref, ebv.at[c], w_ss.at[1], w_rs.at[1], "c", 1)

    def push_weights():
        enc_push.start()
        eb_push.start()
        each_k(lambda k: dec_push(k).start())

    pl.when(c == 1)(push_weights)

    def take_y(i):
        gy(i).wait_recv()
        spread_z(i)

    def take_z(j):
        gz(j).wait_recv()
        spread(j)

    take_z(1), take_z(7), take_y(1), take_y(3), take_z(2), take_z(6), take_y(2), take_z(3), take_z(5), take_z(4)

    @pl.when(c == 0)
    def _():
        pl.semaphore_wait(partner_sem, 1)
        push_weights()

    def all_across(i):
        block = xg.at[y, :, :, hi]
        return remote(block, block, by_ss.at[0], by_rs.at[i - 1], "y", i)

    def all_along(i):
        block = xg.at[:, z, :, lo]
        return remote(block, block, az_ss.at[0], az_rs.at[i - 1], "z", i)

    for i in (1, 3, 2):
        all_across(i).wait_recv()
    for i in (1, 7, 2, 6, 3, 5, 4):
        all_along(i).wait_recv()
    for cp in locals_:
        cp.wait()
    enc_push.wait_recv()
    eb_push.wait_recv()

    rows = xg[...].astype(jnp.float32).reshape(Z * Y * ROWS, D).astype(jnp.bfloat16)
    for side in range(C):
        for n in range(FEATS // TILE):
            at = pl.ds(n * TILE, TILE)
            pre = jnp.dot(rows, wenc[side, :, at], preferred_element_type=jnp.float32) + ebv[side, :, at]
            act[:, pl.ds(side * FEATS + n * TILE, TILE)] = jnp.maximum(pre, 0.0).astype(jnp.bfloat16)

    def product(k, col):
        at = pl.ds(col, TILE)
        weight = wdec[k, :, :, at].reshape(C * FEATS, TILE)
        out = jnp.dot(act[...], weight, preferred_element_type=jnp.float32)
        return out.reshape(Y, Z, ROWS, TILE)

    ready = set()

    def dec_ready(k):
        if k not in ready:
            ready.add(k)
            dec_local(k).wait()
            dec_push(k).wait_recv()

    def move(i, n):
        at = pl.ds(n * TILE, TILE)
        return remote(mvs.at[i, :, :, :, at], mvr.at[i, :, :, :, at], mv_ss.at[i], mv_rs.at[i, n], "x", 1 - 2 * i)

    def moved(k):
        i = k // 2
        dec_ready(k)
        for n in (0, 1, 2, 3):
            mvs[i, :, :, :, pl.ds(n * TILE, TILE)] = product(k, B_COLS + n * TILE).astype(jnp.bfloat16)
            move(i, n).start()

    def own1(g, k, d):
        cols = pl.ds(g.start, g.width)
        return part[k, d, :, :, cols] if g.first == "y" else part[k, :, d, :, cols]

    def own2(g, j, d):
        return g.t[j, d]

    def copy1(g, j, slot, step):
        return remote(g.s1.at[j, slot], g.r1.at[j, slot], g.ss1.at[j], g.rs1.at[j, slot], g.first, step)

    def copy2(g, j, slot, step):
        return remote(g.s2.at[j, slot], g.r2.at[j, slot], g.ss2.at[j], g.rs2.at[j, 0 if g.direct else slot], g.second, step)

    def stage_of(g, stage, j, k):
        if stage == 1:
            return g.first, g.n1, (lambda d: own1(g, k, d)), g.s1, g.r1, (lambda slot, step: copy1(g, j, slot, step))
        return g.second, g.n2, (lambda d: own2(g, j, d)), g.s2, g.r2, (lambda slot, step: copy2(g, j, slot, step))

    done = {}

    def chain_step(i, stage, k, long, s):
        g = gs[i]
        j = k if g.ks == X else k // 2
        axis, size, own, sref, rref, copy = stage_of(g, stage, j, k)
        half = size // 2
        hops, base = (half, 0) if long else (half - 1, half)
        step = (1 if j % 2 == 0 else -1) * (1 if long else -1)
        if s > 0:
            copy(base + s - 1, step).wait_recv()
        if s < hops:
            msg = own(shifted(axis, step * (hops - s)))
            if s > 0:
                msg = msg + rref[j, base + s - 1].astype(jnp.float32)
            sref[j, base + s] = msg.astype(jnp.bfloat16)
            copy(base + s, step).start()
            return
        done[i, stage, k] = done.get((i, stage, k), 0) + 1
        if done[i, stage, k] == 2:
            total = own(lax.axis_index(axis)) + rref[j, half - 1].astype(jnp.float32) + rref[j, size - 2].astype(jnp.float32)
            if stage == 2:
                fin[k, :, pl.ds(g.start, g.width)] = total
                return
            g.t[j] = total
            if g.direct:
                direct_send(g, j)
            else:
                begin(i, 2, k)

    def begin(i, stage, k):
        chain_step(i, stage, k, True, 0)
        chain_step(i, stage, k, False, 0)

    def direct_send(g, j):
        for o in sorted(range(1, g.n2), key=lambda o: -min(o, g.n2 - o)):
            g.s2[j, o - 1] = own2(g, j, shifted(g.second, o)).astype(jnp.bfloat16)
            copy2(g, j, o - 1, o).start()

    def direct_sum(i, k):
        g = gs[i]
        j = k if g.ks == X else k // 2
        remote(g.s2.at[j], g.r2.at[j], g.ss2.at[j], g.rs2.at[j, 0], g.second, 1).wait_recv()
        total = own2(g, j, lax.axis_index(g.second))
        for o in range(1, g.n2):
            total = total + g.r2[j, o - 1].astype(jnp.float32)
        fin[k, :, pl.ds(g.start, g.width)] = total

    def low_columns(k):
        dec_ready(k)
        for n in range(B_COLS // TILE):
            part[k, :, :, :, pl.ds(n * TILE, TILE)] = product(k, n * TILE)
        begin(0, 1, k)
        begin(1, 1, k)

    def high_columns(k):
        dec_ready(k)
        for n in range(A_COLS // TILE):
            at = B_COLS + n * TILE
            part[k, :, :, :, pl.ds(at, TILE)] = product(k, at)
        if k:
            begin(2, 1, k)

    def join(i, n):
        move(i, n).wait_recv()
        at = pl.ds(B_COLS + n * TILE, TILE)
        part[0, :, :, :, at] = part[0, :, :, :, at] + mvr[i, :, :, :, pl.ds(n * TILE, TILE)].astype(jnp.float32)

    def own_target(i):
        tiles = range((gs[i].start - B_COLS) // TILE, (gs[i].start - B_COLS + gs[i].width) // TILE)
        pl.when(l > 0)(lambda: [join(0, n) for n in tiles] and None)
        pl.when(l == X - 1)(lambda: [join(1, n) for n in tiles] and None)
        begin(i, 1, 0)

    def late(k, is_a):
        at = pl.ds(B_COLS, A_COLS) if is_a else pl.ds(0, B_COLS)
        slot = 3 if is_a else k - 1
        return remote(fsend.at[k - 1, :, at], frecv.at[k - 1, :, at], f_ss.at[slot], f_rs.at[slot], "x", k)

    def send_late(k, is_a):
        at = pl.ds(B_COLS, A_COLS) if is_a else pl.ds(0, B_COLS)
        fsend[k - 1, :, at] = fin[k, :, at].astype(jnp.bfloat16)
        late(k, is_a).start()

    left = {(k, is_a): 1 if is_a else 2 for k in range(X) for is_a in (False, True)}

    def run(kind, *rest):
        k = rest[2] if kind == 4 else rest[1] if kind == 5 else 0 if kind == 3 else rest[0]

        def act_():
            if kind == 0:
                low_columns(k)
            elif kind == 1:
                moved(k)
            elif kind == 2:
                high_columns(k)
            elif kind == 3:
                own_target(rest[0])
            else:
                if kind == 4:
                    chain_step(*rest)
                else:
                    direct_sum(*rest)
                i = rest[0]
                last = kind == 5 or (rest[1] == 2 and done.get((i, 2, k), 0) == 2)
                if last:
                    left[k, i >= 2] -= 1
                    if k and not left[k, i >= 2]:
                        send_late(k, i >= 2)

        if k == 0:
            act_()
        else:
            pl.when(l + k < X)(act_)

    for step in ORDER:
        run(*step)

    def take_late(k, is_a):
        late(k, is_a).wait_recv()
        at = pl.ds(B_COLS, A_COLS) if is_a else pl.ds(0, B_COLS)
        fin[0, :, at] = fin[0, :, at] + frecv[k - 1, :, at].astype(jnp.float32)

    for k in (1, 2, 3):
        pl.when(l >= k)(lambda k=k: take_late(k, False))
    pl.when(l >= 2)(lambda: take_late(2, True))
    o_ref[0] = (fin[0] + db_ref[...]).astype(jnp.bfloat16)

    def left_all(src, send, recv):
        remote(src, src, send, recv, "y", 1).wait_send()

    left_all(xg.at[0, pl.ds(0, 3), :, lo], ay_ss.at[0], ay_rs.at[0])
    left_all(xg.at[:, pl.ds(0, 7), :, lo], az_ss.at[0], az_rs.at[0])
    left_all(xg.at[0, pl.ds(0, 7), :, hi], bz_ss.at[0], bz_rs.at[0])
    left_all(xg.at[pl.ds(0, 3), :, :, hi], by_ss.at[0], by_rs.at[0])
    enc_push.wait_send()
    eb_push.wait_send()
    each_k(lambda k: dec_push(k).wait_send())
    each_k(lambda k: left_all(mvs.at[k // 2], mv_ss.at[k // 2], mv_rs.at[k // 2, 0]), (1, 3))
    each_k(lambda k: late(k, False).wait_send(), (1, 2, 3))
    pl.when(l < 2)(lambda: late(2, True).wait_send())

    def drain(g, j):
        left_all(g.s1.at[j], g.ss1.at[j], g.rs1.at[j, 0])
        left_all(g.s2.at[j], g.ss2.at[j], g.rs2.at[j, 0])

    each_k(lambda k: [drain(g, k if g.ks == X else k // 2) for g in gs if g.ks == X or k % 2 == 0] and None)


def per_device(resid_in, enc_weight, enc_bias, dec_weight, dec_bias):
    dma = pltpu.SemaphoreType.DMA
    scratch = [
        pltpu.VMEM((C, D, FEATS), jnp.bfloat16),
        pltpu.VMEM((X, C, FEATS, D), jnp.bfloat16),
        pltpu.VMEM((C, 1, FEATS), jnp.float32),
        pltpu.VMEM((Y, Z, ROWS, D), jnp.bfloat16),
        pltpu.VMEM((Z * Y * ROWS, C * FEATS), jnp.bfloat16),
        pltpu.VMEM((X, Y, Z, ROWS, D), jnp.float32),
        pltpu.VMEM((2, Y, Z, ROWS, A_COLS), jnp.bfloat16),
        pltpu.VMEM((2, Y, Z, ROWS, A_COLS), jnp.bfloat16),
        pltpu.VMEM((X, ROWS, D), jnp.float32),
        pltpu.VMEM((X - 1, ROWS, D), jnp.bfloat16),
        pltpu.VMEM((X - 1, ROWS, D), jnp.bfloat16),
        dma((7,)),
        dma((6,)), dma((6,)),
        dma((1,)), dma((3,)),
        dma((1,)), dma((7,)),
        dma((1,)), dma((7,)),
        dma((1,)), dma((3,)),
        dma((2,)), dma((2, A_COLS // TILE)),
        dma((4,)), dma((4,)),
        pltpu.SemaphoreType.REGULAR,
    ]
    for g in groups():
        scratch += g.scratch()
    anywhere = pl.BlockSpec(memory_space=pl.ANY)
    return pl.pallas_call(
        kernel,
        out_shape=jax.ShapeDtypeStruct((1, ROWS, D), jnp.bfloat16),
        in_specs=[anywhere, anywhere, anywhere, anywhere, pl.BlockSpec(memory_space=pltpu.VMEM)],
        out_specs=pl.BlockSpec(memory_space=pltpu.VMEM),
        scratch_shapes=scratch,
        compiler_params=pltpu.CompilerParams(collective_id=0, has_side_effects=True, vmem_limit_bytes=67043328),
        name="transcoder",
    )(resid_in, enc_weight, enc_bias, dec_weight, dec_bias)


def solution(mesh):
    finer = Mesh(mesh.devices.reshape(Z, Y, C, X), ("z", "y", "c", "x"))
    return jax.shard_map(
        per_device,
        mesh=finer,
        in_specs=(
            P("x", FEAT, None),
            P("x", None, FEAT),
            P("x", FEAT),
            P("x", None, FEAT, None),
            P("x", None),
        ),
        out_specs=P("x", FEAT, None),
        check_vma=False,
    )
```

time: 76.9 us -> 64.1 us (0.83)
  the two profiles are of different devices: /device:TPU:4 before, /device:TPU:6 now
where the time goes in v2:
time: 64.1 us; the launch traced here: 63.9 us
  Pallas kernels  62.5 us (98%)
  local copies, waits for them, and re-layouts  1.39 us (2%)
    pallas_call x1, Pallas kernels, per_device(): pl.pallas_call(kernel, out_shape=jax.ShapeDtypeStruct((1, ROWS, D), jnp.b...  62.5 us
    unnamed x1, local copies, waits for them, and re-layouts  1.39 us

profile of v2, /device:TPU:6, one launch (start us, length us, event | category | flops | bytes accessed | tf_op | source)
XLA Modules:
  0.0 63.9 jit_solution(10647929387798848484)
XLA Ops:
  0.0 62.5 %transcoder.1 = bf16[1,8,2304]{2,1,0:T(8,128)(2,1)} custom-call(bf16[1,8,2304]{2,1,0:T(8,128)(2,1)} %x_ref.1, bf16[1,2304,512]{2,1,0:T(8,128)(2,1)} %enc_ref.1, f32[1,512]{1,0:T(1,128)} %eb_ref.1, bf16[1,4,512,2304]{3,2,1,0:T(8,128)(2,1)} %dec_ref.1, f32[1,2304]{1,0:T(1,128)} %db_ref.1), custom_call_target="tpu_custom_call" | custom-call | tf_op jit(solution)/shard_map/transcoder/pallas_call | solution.py:423
  62.5 1.4 %copy.7 = bf16[1,8,2304]{2,1,0:T(8,128)(2,1)} copy(bf16[1,8,2304]{2,1,0:T(8,128)(2,1)} %transcoder.1) | data formatting | bytes 73728

commit v3 on v2

--- a/solution.py
+++ b/solution.py
@@ -14,7 +14,7 @@
 D = 2304
 FEATS = 512
 TILE = 256
-GATHER_SPLIT = 896
+GATHER_SPLIT = 768
 B_COLS = 1280
 A_COLS = D - B_COLS
 
@@ -103,7 +103,7 @@
     each_k(lambda k: dec_local(k).start())
 
     bar = pltpu.get_barrier_semaphore()
-    peers = [("y", i) for i in (1, 2, 3)] + [("z", i) for i in range(1, 8)] + [("x", i) for i in (1, 2, 3)]
+    peers = [("y", i) for i in (1, 2, 3)] + [("z", i) for i in (1, 2, 6, 7)] + [("x", i) for i in (1, 2, 3)]
 
     @pl.when(c == 0)
     def _():
@@ -122,19 +122,31 @@
     def gy(i):
         return remote(x_ref.at[0, :, lo], xg.at[y, z, :, lo], ay_ss.at[0], ay_rs.at[i - 1], "y", i)
 
-    def gz(i):
-        return remote(x_ref.at[0, :, hi], xg.at[y, z, :, hi], bz_ss.at[0], bz_rs.at[i - 1], "z", i)
-
-    def along(j, i):
-        yb = shifted("y", -j)
-        src = x_ref.at[0, :, lo] if j == 0 else xg.at[yb, z, :, lo]
-        return remote(src, xg.at[yb, z, :, lo], az_ss.at[0], az_rs.at[i - 1], "z", i)
-
-    far_first = (4, 3, 5, 2, 6, 1, 7)
+    def high(off, step):
+        zb = shifted("z", -off)
+        at = lax.rem(off + step + 2 * Z, Z) - 1
+        return remote(xg.at[y, zb, :, hi], xg.at[y, zb, :, hi], bz_ss.at[0], bz_rs.at[at], "z", step)
+
+    def own_high(step):
+        return remote(x_ref.at[0, :, hi], xg.at[y, z, :, hi], bz_ss.at[0], bz_rs.at[step % Z - 1], "z", step)
+
+    def low(j, off, step):
+        yb, zb = shifted("y", -j), shifted("z", -off)
+        src = x_ref.at[0, :, lo] if j == 0 and off == 0 else xg.at[yb, zb, :, lo]
+        to = (off + step) % Z
+        at = 7 + (to == 6) * 4 + j if to in (2, 6) else to - 1
+        return remote(src, xg.at[yb, zb, :, lo], az_ss.at[0], az_rs.at[at], "z", step)
 
     def spread_z(j):
-        for i in far_first:
-            along(j, i).start()
+        for step in (2, -2, 1, -1):
+            low(j, 0, step).start()
+
+    def relay_low(j):
+        for sign in (1, -1):
+            low(j, 0, 2 * sign).wait_recv()
+            long = sign == (1 if j % 2 == 0 else -1)
+            for step in (2, 1) if long else (1,):
+                low(j, 2 * sign, step * sign).start()
 
     def across(j, i):
         zb = shifted("z", -j)
@@ -147,8 +159,8 @@
 
     for i in (1, 3, 2):
         gy(i).start()
-    for i in far_first:
-        gz(i).start()
+    for step in (2, -2, 1, -1):
+        own_high(step).start()
     spread(0)
     spread_z(0)
 
@@ -160,22 +172,35 @@
         eb_push.start()
         each_k(lambda k: dec_push(k).start())
 
-    pl.when(c == 1)(push_weights)
+    @pl.when(c == 0)
+    def _():
+        pl.semaphore_wait(partner_sem, 1)
+
+    push_weights()
 
     def take_y(i):
         gy(i).wait_recv()
         spread_z(i)
 
-    def take_z(j):
-        gz(j).wait_recv()
-        spread(j)
-
-    take_z(1), take_z(7), take_y(1), take_y(3), take_z(2), take_z(6), take_y(2), take_z(3), take_z(5), take_z(4)
-
-    @pl.when(c == 0)
-    def _():
-        pl.semaphore_wait(partner_sem, 1)
-        push_weights()
+    turn = 1 - 2 * lax.rem(y, 2)
+
+    def take_z(off):
+        own_high(off).wait_recv()
+        spread(off)
+
+    def relay_z(off):
+        own_high(off).wait_recv()
+        sign = 1 if off == 2 else -1
+        high(2 * sign, sign).start()
+
+        @pl.when(turn == sign)
+        def _():
+            high(2 * sign, 2 * sign).start()
+
+        spread(off)
+
+    take_z(1), take_z(7), take_y(1), take_y(3), relay_z(2), relay_z(6), relay_low(0), take_y(2), relay_low(1), relay_low(3)
+    take_z(3), take_z(5), take_z(4), relay_low(2)
 
     def all_across(i):
         block = xg.at[y, :, :, hi]
@@ -187,7 +212,7 @@
 
     for i in (1, 3, 2):
         all_across(i).wait_recv()
-    for i in (1, 7, 2, 6, 3, 5, 4):
+    for i in (1, 7, 3, 5, 4):
         all_along(i).wait_recv()
     for cp in locals_:
         cp.wait()
@@ -410,7 +435,7 @@
         dma((7,)),
         dma((6,)), dma((6,)),
         dma((1,)), dma((3,)),
-        dma((1,)), dma((7,)),
+        dma((1,)), dma((15,)),
         dma((1,)), dma((7,)),
         dma((1,)), dma((3,)),
         dma((2,)), dma((2, A_COLS // TILE)),

time: 64.1 us -> 62 us (0.967)
  Pallas kernels: 62.5 us -> 60.4 us
    pallas_call x1, Pallas kernels: 62.5 us -> 60.4 us  [per_device(): pl.pallas_call(kernel, out_shape=jax.ShapeDtypeStruct((1, ROWS, D), jnp.b...]
where the time goes in v3:
time: 62 us; the launch traced here: 61.8 us
  Pallas kernels  60.4 us (97%)
  local copies, waits for them, and re-layouts  1.39 us (2%)
    pallas_call x1, Pallas kernels, per_device(): pl.pallas_call(kernel, out_shape=jax.ShapeDtypeStruct((1, ROWS, D), jnp.b...  60.4 us
    unnamed x1, local copies, waits for them, and re-layouts  1.39 us

profile of v3, /device:TPU:6, one launch (start us, length us, event | category | flops | bytes accessed | tf_op | source)
XLA Modules:
  0.0 61.8 jit_solution(6976256186429451730)
XLA Ops:
  0.0 60.4 %transcoder.1 = bf16[1,8,2304]{2,1,0:T(8,128)(2,1)} custom-call(bf16[1,8,2304]{2,1,0:T(8,128)(2,1)} %x_ref.1, bf16[1,2304,512]{2,1,0:T(8,128)(2,1)} %enc_ref.1, f32[1,512]{1,0:T(1,128)} %eb_ref.1, bf16[1,4,512,2304]{3,2,1,0:T(8,128)(2,1)} %dec_ref.1, f32[1,2304]{1,0:T(1,128)} %db_ref.1), custom_call_target="tpu_custom_call" | custom-call | tf_op jit(solution)/shard_map/transcoder/pallas_call | solution.py:448
  60.4 1.4 %copy.7 = bf16[1,8,2304]{2,1,0:T(8,128)(2,1)} copy(bf16[1,8,2304]{2,1,0:T(8,128)(2,1)} %transcoder.1) | data formatting | bytes 73728

commit v4 on v3

--- a/solution.py
+++ b/solution.py
@@ -19,13 +19,13 @@
 A_COLS = D - B_COLS
 
 ORDER = (
-    (1,1), (1,3), (0,1), (0,2), (2,2), (0,3), (0,0), (4,1,1,1,1,1), (4,1,1,1,0,1), (4,0,1,1,1,1), (4,0,1,1,0,1), (2,0), (4,1,1,2,1,1),
-    (4,1,1,2,0,1), (4,0,1,2,1,1), (4,0,1,2,0,1), (4,1,1,3,1,1), (4,1,1,3,0,1), (4,1,1,0,1,1), (4,1,1,0,0,1), (4,2,1,2,1,1),
-    (4,2,1,2,0,1), (4,1,1,1,1,2), (4,1,1,1,0,2), (4,1,1,2,1,2), (4,1,1,2,0,2), (4,0,1,3,1,1), (4,0,1,3,0,1), (4,1,1,3,1,2),
-    (4,1,1,3,0,2), (3,2), (4,0,1,0,1,1), (4,0,1,0,0,1), (4,1,1,0,1,2), (4,1,1,0,0,2), (4,0,1,1,1,2), (4,0,1,2,1,2), (4,1,1,1,1,3),
-    (4,1,1,1,0,3), (4,1,1,2,1,3), (4,1,1,2,0,3), (4,1,1,3,1,3), (4,1,1,3,0,3), (4,2,1,2,1,2), (4,1,1,0,1,3), (4,1,1,0,0,3),
-    (4,2,1,0,1,1), (4,0,1,3,1,2), (4,0,1,0,1,2), (5,0,1), (4,2,1,0,0,1), (4,1,1,1,1,4), (4,1,1,2,1,4), (5,0,2), (4,1,1,3,1,4),
-    (4,2,1,0,1,2), (4,1,1,0,1,4), (5,1,1), (5,1,2), (5,1,3), (5,2,2), (5,1,0), (5,0,3), (5,0,0), (5,2,0),
+    (0,1), (1,1), (1,3), (4,1,1,1,1,1), (4,1,1,1,0,1), (4,0,1,1,1,1), (4,0,1,1,0,1), (0,3), (0,2), (2,2), (4,1,1,1,1,2),
+    (4,1,1,1,0,2), (0,0), (4,0,1,1,1,2), (4,1,1,3,1,1), (4,1,1,3,0,1), (2,0), (4,0,1,3,0,1), (4,0,1,3,1,1), (4,1,1,2,1,1),
+    (4,1,1,2,0,1), (4,0,1,2,1,1), (4,0,1,2,0,1), (4,1,1,1,1,3), (4,1,1,1,0,3), (4,1,1,0,1,1), (4,1,1,0,0,1), (4,2,1,2,0,1),
+    (4,2,1,2,1,1), (4,1,1,3,0,2), (3,2), (4,0,1,0,1,1), (4,1,1,3,1,2), (4,0,1,0,0,1), (4,1,1,2,1,2), (5,0,1), (4,1,1,2,0,2),
+    (4,0,1,2,1,2), (4,1,1,0,1,2), (4,0,1,3,1,2), (4,1,1,1,1,4), (4,1,1,3,0,3), (4,1,1,0,0,2), (4,1,1,2,1,3), (4,1,1,3,1,3),
+    (4,2,1,2,1,2), (4,2,1,0,1,1), (4,1,1,2,0,3), (4,0,1,0,1,2), (4,1,1,0,1,3), (4,2,1,0,0,1), (5,0,2), (4,1,1,2,1,4), (5,1,1),
+    (4,1,1,0,0,3), (5,0,3), (4,2,1,0,1,2), (4,1,1,3,1,4), (5,1,2), (4,1,1,0,1,4), (5,1,3), (5,2,2), (5,0,0), (5,1,0), (5,2,0),
 )
 
 class Group:
@@ -199,7 +199,7 @@
 
         spread(off)
 
-    take_z(1), take_z(7), take_y(1), take_y(3), relay_z(2), relay_z(6), relay_low(0), take_y(2), relay_low(1), relay_low(3)
+    take_y(1), take_y(3), take_z(1), take_z(7), relay_z(2), relay_z(6), relay_low(0), take_y(2), relay_low(1), relay_low(3)
     take_z(3), take_z(5), take_z(4), relay_low(2)
 
     def all_across(i):

time: 62 us -> 61.3 us (0.989)
  Pallas kernels: 60.4 us -> 59.3 us
    pallas_call x1, Pallas kernels: 60.4 us -> 59.3 us  [per_device(): pl.pallas_call(kernel, out_shape=jax.ShapeDtypeStruct((1, ROWS, D), jnp.b...]
where the time goes in v4:
time: 61.3 us; the launch traced here: 60.7 us
  Pallas kernels  59.3 us (97%)
  local copies, waits for them, and re-layouts  1.39 us (2%)
    pallas_call x1, Pallas kernels, per_device(): pl.pallas_call(kernel, out_shape=jax.ShapeDtypeStruct((1, ROWS, D), jnp.b...  59.3 us
    unnamed x1, local copies, waits for them, and re-layouts  1.39 us

profile of v4, /device:TPU:6, one launch (start us, length us, event | category | flops | bytes accessed | tf_op | source)
XLA Modules:
  0.0 60.7 jit_solution(15057249175159627548)
XLA Ops:
  0.0 59.3 %transcoder.1 = bf16[1,8,2304]{2,1,0:T(8,128)(2,1)} custom-call(bf16[1,8,2304]{2,1,0:T(8,128)(2,1)} %x_ref.1, bf16[1,2304,512]{2,1,0:T(8,128)(2,1)} %enc_ref.1, f32[1,512]{1,0:T(1,128)} %eb_ref.1, bf16[1,4,512,2304]{3,2,1,0:T(8,128)(2,1)} %dec_ref.1, f32[1,2304]{1,0:T(1,128)} %db_ref.1), custom_call_target="tpu_custom_call" | custom-call | tf_op jit(solution)/shard_map/transcoder/pallas_call | solution.py:448
  59.3 1.4 %copy.7 = bf16[1,8,2304]{2,1,0:T(8,128)(2,1)} copy(bf16[1,8,2304]{2,1,0:T(8,128)(2,1)} %transcoder.1) | data formatting | bytes 73728

commit v5 on v4

--- a/solution.py
+++ b/solution.py
@@ -20,12 +20,12 @@
 
 ORDER = (
     (0,1), (1,1), (1,3), (4,1,1,1,1,1), (4,1,1,1,0,1), (4,0,1,1,1,1), (4,0,1,1,0,1), (0,3), (0,2), (2,2), (4,1,1,1,1,2),
-    (4,1,1,1,0,2), (0,0), (4,0,1,1,1,2), (4,1,1,3,1,1), (4,1,1,3,0,1), (2,0), (4,0,1,3,0,1), (4,0,1,3,1,1), (4,1,1,2,1,1),
+    (4,1,1,1,0,2), (0,0), (4,0,1,1,1,2), (4,1,1,3,1,1), (4,1,1,3,0,1), (4,0,1,3,0,1), (4,0,1,3,1,1), (2,0), (4,1,1,2,1,1),
     (4,1,1,2,0,1), (4,0,1,2,1,1), (4,0,1,2,0,1), (4,1,1,1,1,3), (4,1,1,1,0,3), (4,1,1,0,1,1), (4,1,1,0,0,1), (4,2,1,2,0,1),
-    (4,2,1,2,1,1), (4,1,1,3,0,2), (3,2), (4,0,1,0,1,1), (4,1,1,3,1,2), (4,0,1,0,0,1), (4,1,1,2,1,2), (5,0,1), (4,1,1,2,0,2),
-    (4,0,1,2,1,2), (4,1,1,0,1,2), (4,0,1,3,1,2), (4,1,1,1,1,4), (4,1,1,3,0,3), (4,1,1,0,0,2), (4,1,1,2,1,3), (4,1,1,3,1,3),
-    (4,2,1,2,1,2), (4,2,1,0,1,1), (4,1,1,2,0,3), (4,0,1,0,1,2), (4,1,1,0,1,3), (4,2,1,0,0,1), (5,0,2), (4,1,1,2,1,4), (5,1,1),
-    (4,1,1,0,0,3), (5,0,3), (4,2,1,0,1,2), (4,1,1,3,1,4), (5,1,2), (4,1,1,0,1,4), (5,1,3), (5,2,2), (5,0,0), (5,1,0), (5,2,0),
+    (4,2,1,2,1,1), (4,1,1,3,0,2), (4,0,1,0,1,1), (4,0,1,0,0,1), (4,1,1,3,1,2), (4,1,1,2,1,2), (3,2), (4,0,1,2,1,2), (4,0,1,3,1,2),
+    (5,0,1), (4,1,1,2,0,2), (4,1,1,0,1,2), (4,1,1,1,1,4), (4,1,1,3,0,3), (4,1,1,0,0,2), (4,0,1,0,1,2), (4,2,1,2,1,2), (4,1,1,2,1,3),
+    (4,1,1,3,1,3), (4,2,1,0,1,1), (4,2,1,0,0,1), (5,0,2), (4,1,1,0,1,3), (4,1,1,2,0,3), (5,1,1), (5,0,3), (4,1,1,0,0,3), (5,0,0),
+    (4,2,1,0,1,2), (4,1,1,2,1,4), (4,1,1,0,1,4), (5,2,2), (4,1,1,3,1,4), (5,1,2), (5,1,0), (5,1,3), (5,2,0),
 )
 
 class Group:

time: 61.3 us -> 63 us (1.028)
  Pallas kernels: 59.3 us -> 61.5 us
    pallas_call x1, Pallas kernels: 59.3 us -> 61.5 us  [per_device(): pl.pallas_call(kernel, out_shape=jax.ShapeDtypeStruct((1, ROWS, D), jnp.b...]
where the time goes in v5:
time: 63 us; the launch traced here: 62.9 us
  Pallas kernels  61.5 us (98%)
  local copies, waits for them, and re-layouts  1.39 us (2%)
    pallas_call x1, Pallas kernels, per_device(): pl.pallas_call(kernel, out_shape=jax.ShapeDtypeStruct((1, ROWS, D), jnp.b...  61.5 us
    unnamed x1, local copies, waits for them, and re-layouts  1.39 us

profile of v5, /device:TPU:6, one launch (start us, length us, event | category | flops | bytes accessed | tf_op | source)
XLA Modules:
  0.0 62.9 jit_solution(3889312530521331048)
XLA Ops:
  0.0 61.5 %transcoder.1 = bf16[1,8,2304]{2,1,0:T(8,128)(2,1)} custom-call(bf16[1,8,2304]{2,1,0:T(8,128)(2,1)} %x_ref.1, bf16[1,2304,512]{2,1,0:T(8,128)(2,1)} %enc_ref.1, f32[1,512]{1,0:T(1,128)} %eb_ref.1, bf16[1,4,512,2304]{3,2,1,0:T(8,128)(2,1)} %dec_ref.1, f32[1,2304]{1,0:T(1,128)} %db_ref.1), custom_call_target="tpu_custom_call" | custom-call | tf_op jit(solution)/shard_map/transcoder/pallas_call | solution.py:448
  61.5 1.4 %copy.7 = bf16[1,8,2304]{2,1,0:T(8,128)(2,1)} copy(bf16[1,8,2304]{2,1,0:T(8,128)(2,1)} %transcoder.1) | data formatting | bytes 73728
